TPU v7x, 32 devices: a whole 2x2x4 slice. The times are simulated.
32 devices in a mesh: wide: 8 (over y, x, core), narrow: 4 (over z).
Axes of the slice: x: 2, y: 2, z: 4, core: 2. Of those that a mesh axis runs over, the one named last changes fastest.
Arguments:
- tokens: bfloat16 [64, 208, 768], P('wide'), may hold values from -6 to 6
- grid_shape: int32 [64, 2], P('wide'), may hold values from 8 to 24, as said below
- first_gain: bfloat16 [768], replicated, may hold values from 0.5 to 1.5
- first_shift: bfloat16 [768], replicated, may hold values from -1.1953125 to 1.1953125
- qkv_weight: bfloat16 [3, 768, 768], P(None, None, 'narrow'), may hold values from -0.21875 to 0.21875
- query_bias: bfloat16 [768], P('narrow'), may hold values from -1.796875 to 1.796875
- value_bias: bfloat16 [768], P('narrow'), may hold values from -0.59765625 to 0.59765625
- rel_table: bfloat16 [12, 2212], P('narrow'), may hold values from -5 to 5
- proj_weight: bfloat16 [768, 768], P('narrow'), may hold values from -1.25 to 1.25
- proj_bias: bfloat16 [768], replicated, may hold values from -1.796875 to 1.796875
- attn_scale: bfloat16 [768], replicated, may hold values from 0.25 to 1.75
- second_gain: bfloat16 [768], replicated, may hold values from 0.5 to 1.5
- second_shift: bfloat16 [768], replicated, may hold values from -1.1953125 to 1.1953125
- up_weight: bfloat16 [768, 3072], P(None, 'narrow'), may hold values from -0.21875 to 0.21875
- up_bias: bfloat16 [3072], P('narrow'), may hold values from -3 to 3
- down_weight: bfloat16 [3072, 768], P('narrow'), may hold values from -0.15625 to 0.15625
- down_bias: bfloat16 [768], replicated, may hold values from -1.796875 to 1.796875
- mlp_scale: bfloat16 [768], replicated, may hold values from 0.25 to 1.75
- cotangent: bfloat16 [64, 208, 768], P('wide'), may hold values from -6 to 6
Outputs:
- layer_out: bfloat16 [64, 208, 768], P('wide')
- tokens_grad: float32 [64, 208, 768], P('wide')
- first_gain_grad: float32 [768], replicated
- first_shift_grad: float32 [768], replicated
- qkv_weight_grad: float32 [3, 768, 768], P(None, None, 'narrow')
- query_bias_grad: float32 [768], P('narrow')
- value_bias_grad: float32 [768], P('narrow')
- rel_table_grad: float32 [12, 2212], P('narrow')
- proj_weight_grad: float32 [768, 768], P('narrow')
- proj_bias_grad: float32 [768], replicated
- attn_scale_grad: float32 [768], replicated
- second_gain_grad: float32 [768], replicated
- second_shift_grad: float32 [768], replicated
- up_weight_grad: float32 [768, 3072], P(None, 'narrow')
- up_bias_grad: float32 [3072], P('narrow')
- down_weight_grad: float32 [3072, 768], P('narrow')
- down_bias_grad: float32 [768], replicated
- mlp_scale_grad: float32 [768], replicated
Inputs may be any that keep to these rules, and one draw needn't show every extreme that they name: `grid_shape`: each row is (height, width) of one image's patch grid, one of 14 x 14, 10 x 20, 20 x 10, 8 x 24, 24 x 8, 12 x 16, 16 x 12, 13 x 15; each of these occurs in every draw.
All inputs are finite; a program needn't handle non-finite values.
Results may differ from a plain program's by a relative error of at most 0.013.
Values sent between devices are 32-bit elements; how exact they have to be, the bound alone decides.
A program may use at most 384 MiB of HBM per device.

v0:
```python
import jax
import jax.numpy as jnp
from jax import lax
from jax.sharding import PartitionSpec as P

HD = 64
MAXG = 24
EPSILON = 1e-06
NEG_LARGE = -1000000000.0
INV_ROOT_TWO = 0.7071067811865476
INV_ROOT_TWO_PI = 0.3989422804014327


def slot_layout(grid_shape, slot_count):
    slot_ids = jnp.arange(slot_count, dtype=jnp.int32)
    patch_ids = slot_ids - 1
    grid_height = grid_shape[:, 0:1]
    grid_width = grid_shape[:, 1:2]
    is_valid = slot_ids[None, :] <= grid_height * grid_width
    row_place = jnp.floor_divide(patch_ids[None, :], grid_width)
    col_place = patch_ids[None, :] - row_place * grid_width
    span_size = 2 * MAXG - 1
    row_delta = row_place[:, :, None] - row_place[:, None, :] + (MAXG - 1)
    col_delta = col_place[:, :, None] - col_place[:, None, :] + (MAXG - 1)
    pair_index = row_delta * span_size + col_delta
    is_patch = jnp.logical_and(slot_ids[None, :] >= 1, is_valid)
    is_class = jnp.broadcast_to(slot_ids[None, :] == 0, is_patch.shape)
    both_patch = jnp.logical_and(is_patch[:, :, None], is_patch[:, None, :])
    class_query = jnp.logical_and(is_class[:, :, None], is_patch[:, None, :])
    class_key = jnp.logical_and(is_patch[:, :, None], is_class[:, None, :])
    last_entry = span_size * span_size
    pair_index = jnp.where(
        both_patch,
        pair_index,
        jnp.where(class_query, last_entry, jnp.where(class_key, last_entry + 1, last_entry + 2)),
    )
    return (pair_index, is_valid)


def norm_stats(values):
    centre = jnp.mean(values, axis=1, keepdims=True)
    centred = values - centre
    inv_root = lax.rsqrt(jnp.mean(centred * centred, axis=1, keepdims=True) + EPSILON)
    return (centred * inv_root, inv_root)


def norm_back(incoming, normed, inv_root, gain):
    scaled = incoming * gain
    return inv_root * (
        scaled
        - jnp.mean(scaled, axis=1, keepdims=True)
        - normed * jnp.mean(scaled * normed, axis=1, keepdims=True)
    )


def gelu_exact(inputs):
    return 0.5 * inputs * (1.0 + lax.erf(inputs * INV_ROOT_TWO))


def gelu_slope(inputs):
    return (
        0.5 * (1.0 + lax.erf(inputs * INV_ROOT_TWO))
        + inputs * jnp.exp(-0.5 * inputs * inputs) * INV_ROOT_TWO_PI
    )


def body(
    tokens,
    grid_shape,
    first_gain,
    first_shift,
    qkv_weight,
    query_bias,
    value_bias,
    rel_table,
    proj_weight,
    proj_bias,
    attn_scale,
    second_gain,
    second_shift,
    up_weight,
    up_bias,
    down_weight,
    down_bias,
    mlp_scale,
    cotangent,
):
    float_type = jnp.float32
    brain_type = jnp.bfloat16
    images, slot_count, model_width = tokens.shape
    local_heads, table_size = rel_table.shape
    head_size = HD
    local_width = local_heads * head_size
    total_rows = images * slot_count
    head_split = (images, slot_count, local_heads, head_size)
    query_scale = head_size ** (-0.5)
    pair_index, is_valid = slot_layout(grid_shape, slot_count)
    key_open = is_valid[:, None, None, :]
    table_f = rel_table.astype(float_type)
    table_bias = jnp.transpose(jnp.take(table_f, pair_index, axis=1), (1, 0, 2, 3))
    first_gain_f = first_gain.astype(float_type)
    second_gain_f = second_gain.astype(float_type)
    attn_scale_f = attn_scale.astype(float_type)
    mlp_scale_f = mlp_scale.astype(float_type)
    flat_in = tokens.reshape(total_rows, model_width).astype(float_type)
    normed_one, inv_one = norm_stats(flat_in)
    first_in = (normed_one * first_gain_f + first_shift.astype(float_type)).astype(brain_type)
    projected = jnp.einsum("rd,cde->cre", first_in, qkv_weight, preferred_element_type=float_type)
    queries = ((projected[0] + query_bias.astype(float_type)) * query_scale).astype(brain_type)
    keys_low = projected[1].astype(brain_type)
    values_low = (projected[2] + value_bias.astype(float_type)).astype(brain_type)
    query_heads = queries.reshape(head_split)
    key_heads = keys_low.reshape(head_split)
    value_heads = values_low.reshape(head_split)

    def attention_scores():
        raw_scores = jnp.einsum(
            "ishd,ithd->ihst", query_heads, key_heads, preferred_element_type=float_type
        )
        return jnp.where(key_open, raw_scores + table_bias, NEG_LARGE)

    scores = attention_scores()
    row_top = jnp.max(scores, axis=-1, keepdims=True)
    log_total = row_top + jnp.log(jnp.sum(jnp.exp(scores - row_top), axis=-1, keepdims=True))
    probs_low = jnp.exp(scores - log_total).astype(brain_type)
    attended = jnp.einsum(
        "ihst,ithd->ishd", probs_low, value_heads, preferred_element_type=float_type
    )
    attended = attended.reshape(total_rows, local_width).astype(brain_type)
    attn_part = jnp.dot(attended, proj_weight, preferred_element_type=float_type)
    attn_branch = lax.psum(attn_part, "narrow") + proj_bias.astype(float_type)
    middle = flat_in + attn_scale_f * attn_branch
    normed_two, inv_two = norm_stats(middle)
    second_in = (normed_two * second_gain_f + second_shift.astype(float_type)).astype(brain_type)
    up_pre = jnp.dot(second_in, up_weight, preferred_element_type=float_type) + up_bias.astype(
        float_type
    )
    hidden_low = gelu_exact(up_pre).astype(brain_type)
    down_part = jnp.dot(hidden_low, down_weight, preferred_element_type=float_type)
    mlp_branch = lax.psum(down_part, "narrow") + down_bias.astype(float_type)
    layer_out = (
        (middle + mlp_scale_f * mlp_branch)
        .astype(brain_type)
        .reshape(images, slot_count, model_width)
    )
    out_grad = cotangent.reshape(total_rows, model_width).astype(float_type) * is_valid.reshape(
        total_rows, 1
    ).astype(float_type)
    mlp_scale_grad = jnp.sum(out_grad * mlp_branch, axis=0)
    down_bias_grad = jnp.sum(out_grad, axis=0) * mlp_scale_f
    branch_low = (out_grad * mlp_scale_f).astype(brain_type)
    down_weight_grad = jnp.einsum(
        "rf,rd->fd", hidden_low, branch_low, preferred_element_type=float_type
    )
    hidden_grad = jnp.einsum(
        "rd,fd->rf", branch_low, down_weight, preferred_element_type=float_type
    )
    pre_low = (hidden_grad * gelu_slope(up_pre)).astype(brain_type)
    up_bias_grad = jnp.sum(pre_low.astype(float_type), axis=0)
    up_weight_grad = jnp.einsum("rd,rf->df", second_in, pre_low, preferred_element_type=float_type)
    second_part = jnp.einsum("rf,df->rd", pre_low, up_weight, preferred_element_type=float_type)
    second_grad = lax.psum(second_part, "narrow")
    second_gain_grad = jnp.sum(second_grad * normed_two, axis=0)
    second_shift_grad = jnp.sum(second_grad, axis=0)
    middle_grad = out_grad + norm_back(second_grad, normed_two, inv_two, second_gain_f)
    attn_scale_grad = jnp.sum(middle_grad * attn_branch, axis=0)
    proj_bias_grad = jnp.sum(middle_grad, axis=0) * attn_scale_f
    attn_low = (middle_grad * attn_scale_f).astype(brain_type)
    proj_weight_grad = jnp.einsum(
        "re,rd->ed", attended, attn_low, preferred_element_type=float_type
    )
    attended_grad = (
        jnp.einsum("rd,ed->re", attn_low, proj_weight, preferred_element_type=float_type)
        .astype(brain_type)
        .reshape(head_split)
    )
    probs_again = jnp.exp(attention_scores() - log_total)
    probs_again_low = probs_again.astype(brain_type)
    prob_grad = jnp.einsum(
        "ishd,ithd->ihst", attended_grad, value_heads, preferred_element_type=float_type
    )
    value_grad = jnp.einsum(
        "ihst,ishd->ithd", probs_again_low, attended_grad, preferred_element_type=float_type
    ).astype(brain_type)
    row_inner = jnp.sum(probs_again * prob_grad, axis=-1, keepdims=True)
    score_grad = probs_again * (prob_grad - row_inner)
    flat_index = pair_index.reshape(-1)
    head_major = jnp.transpose(score_grad, (1, 0, 2, 3)).reshape(local_heads, -1)
    rel_table_grad = jax.vmap(
        lambda entries: jax.ops.segment_sum(entries, flat_index, num_segments=table_size)
    )(head_major)
    score_low = score_grad.astype(brain_type)
    query_grad = jnp.einsum(
        "ihst,ithd->ishd", score_low, key_heads, preferred_element_type=float_type
    ).astype(brain_type) * jnp.asarray(query_scale, brain_type)
    key_grad = jnp.einsum(
        "ihst,ishd->ithd", score_low, query_heads, preferred_element_type=float_type
    ).astype(brain_type)
    query_grad = query_grad.reshape(total_rows, local_width)
    key_grad = key_grad.reshape(total_rows, local_width)
    value_grad = value_grad.reshape(total_rows, local_width)
    query_bias_grad = jnp.sum(query_grad.astype(float_type), axis=0)
    value_bias_grad = jnp.sum(value_grad.astype(float_type), axis=0)
    stacked_grads = jnp.stack([query_grad, key_grad, value_grad])
    qkv_weight_grad = jnp.einsum(
        "rd,cre->cde", first_in, stacked_grads, preferred_element_type=float_type
    )
    first_part = jnp.einsum(
        "cre,cde->rd", stacked_grads, qkv_weight, preferred_element_type=float_type
    )
    first_grad = lax.psum(first_part, "narrow")
    first_gain_grad = jnp.sum(first_grad * normed_one, axis=0)
    first_shift_grad = jnp.sum(first_grad, axis=0)
    tokens_grad = (middle_grad + norm_back(first_grad, normed_one, inv_one, first_gain_f)).reshape(
        images, slot_count, model_width
    )
    (
        first_gain_grad,
        first_shift_grad,
        qkv_weight_grad,
        query_bias_grad,
        value_bias_grad,
        rel_table_grad,
        proj_weight_grad,
        proj_bias_grad,
        attn_scale_grad,
        second_gain_grad,
        second_shift_grad,
        up_weight_grad,
        up_bias_grad,
        down_weight_grad,
        down_bias_grad,
        mlp_scale_grad,
    ) = lax.psum(
        (
            first_gain_grad,
            first_shift_grad,
            qkv_weight_grad,
            query_bias_grad,
            value_bias_grad,
            rel_table_grad,
            proj_weight_grad,
            proj_bias_grad,
            attn_scale_grad,
            second_gain_grad,
            second_shift_grad,
            up_weight_grad,
            up_bias_grad,
            down_weight_grad,
            down_bias_grad,
            mlp_scale_grad,
        ),
        "wide",
    )
    return (
        layer_out,
        tokens_grad,
        first_gain_grad,
        first_shift_grad,
        qkv_weight_grad,
        query_bias_grad,
        value_bias_grad,
        rel_table_grad,
        proj_weight_grad,
        proj_bias_grad,
        attn_scale_grad,
        second_gain_grad,
        second_shift_grad,
        up_weight_grad,
        up_bias_grad,
        down_weight_grad,
        down_bias_grad,
        mlp_scale_grad,
    )


def solution(mesh):
    return jax.shard_map(
        body,
        mesh=mesh,
        in_specs=(
            P("wide", None, None),
            P("wide", None),
            P(),
            P(),
            P(None, None, "narrow"),
            P("narrow"),
            P("narrow"),
            P("narrow", None),
            P("narrow", None),
            P(),
            P(),
            P(),
            P(),
            P(None, "narrow"),
            P("narrow"),
            P("narrow", None),
            P(),
            P(),
            P("wide", None, None),
        ),
        out_specs=(
            P("wide", None, None),
            P("wide", None, None),
            P(),
            P(),
            P(None, None, "narrow"),
            P("narrow"),
            P("narrow"),
            P("narrow", None),
            P("narrow", None),
            P(),
            P(),
            P(),
            P(),
            P(None, "narrow"),
            P("narrow"),
            P("narrow", None),
            P(),
            P(),
        ),
        check_vma=False,
    )
```

profile of v0, /device:TPU:4, one launch (start us, length us, event | category | flops | bytes accessed | tf_op | source)
XLA Modules:
  0.0 3937.0 jit_solution(91646839557959551)
XLA Ops:
  25.9 3.4 reshape.864
  34.3 3.5 squeeze.7
  37.8 3.2 squeeze.8
  41.0 1253.0 %gather_fusion = f32[346112,3]{1,0:T(8,128)} fusion(f32[3,2212]{0,1:T(8,128)S(1)} %copy.53, s32[346112]{0:T(1024)} %broadcast_clamp_fusion), kind=kCustom, calls=%fused_computation | custom fusion | bytes 9691136 | tf_op jit(solution)/shard_map/jit(_take)/gather | solution.py:100
  1294.0 102.1 %copy.55 = f32[8,208,208,3]{1,2,3,0:T(8,128)} copy(f32[8,208,208,3]{3,2,1,0:T(8,128)} %bitcast.9) | data formatting | bytes 8306688 | tf_op jit(solution)/shard_map/jit(_take)/gather | solution.py:100
  1396.1 5.7 fusion.61
  1408.8 4.1 fusion.65
  1413.8 3.9 multiply_convert_fusion.2
  1417.7 181.4 %all-reduce.8.cloned.1.call-done = f32[1664,768]{1,0:T(8,128)} async-done(((f32[1664,768]{1,0:T(8,128)}), f32[1664,768]{1,0:T(8,128)}) %all-reduce.8.cloned.1.call-update) | async-done | bytes 5111824 | tf_op jit(solution)/shard_map/psum | solution.py:131
  1599.0 4.2 fusion.60
  1606.6 6.7 multiply_convert_fusion.3
  1613.3 4.7 convert_reduce_fusion.1
  1619.5 4.4 fusion.67
  1625.2 6.2 fusion.66
  1631.4 176.4 %all-reduce.10.cloned.1.call-done = f32[1664,768]{1,0:T(8,128)} async-done(((f32[1664,768]{1,0:T(8,128)}), f32[1664,768]{1,0:T(8,128)}) %all-reduce.10.cloned.1.call-update) | async-done | bytes 5111824 | tf_op jit(solution)/shard_map/psum | solution.py:162
  1807.8 5.3 multiply_reduce_fusion.2
  1814.0 6.0 multiply_reduce_fusion.3
  1826.7 3.7 convert_reduce_fusion.2
  1830.4 4.3 multiply_reduce_fusion.4
  1848.6 4.4 convolution_bitcast_fusion
  1861.2 5.7 fusion.69
  1866.9 3.8 fusion.68
  1870.9 4.1 fusion.39
  1879.1 8.8 fusion.6
  1887.9 6.2 copy.67
  1894.1 10.1 reshape.871
  1904.2 76.8 %copy.68 = f32[346112,3]{1,0:T(8,128)} copy(f32[346112,3]{0,1:T(4,128)} %bitcast.148) | data formatting | bytes 8306688 | tf_op jit(solution)/shard_map/reshape | solution.py:188
  1981.0 1865.8 %scatter_custom_fusion = f32[3,2212]{0,1:T(8,128)S(1)} fusion(s32[346112]{0:T(1024)S(1)} %reshape.872, f32[346112,3]{1,0:T(8,128)} %copy.68, f32[]{:T(128)} %constant.22.clone.1), kind=kCustom, calls=%fused_computation.92 | custom fusion | flops 1038336 | bytes 27056 | tf_op jit(solution)/shard_map/vmap()/scatter-add | solution.py:190
  3847.0 5.6 fusion.24
  3852.6 4.6 multiply_reduce_fusion
  3857.2 57.1 %all-reduce = (f32[768]{0:T(1024)}, f32[768]{0:T(1024)}, f32[192]{0:T(256)}, f32[192]{0:T(256)}, f32[3,2212]{0,1:T(8,128)S(1)}, /*index=5*/f32[768]{0:T(1024)}, ...) all-reduce(f32[768]{0:T(1024)S(1)} %get-tuple-element.56, ...), channel_id=1, replica_groups=mesh['wide'=8,'narrow'=4] {'wide'}, use_global_device_ids=true, to_apply=%region_16.17 | all-reduce | flops 13932 | bytes 111456 | tf_op jit(solution)/shard_map/psum | solution.py:234
  3915.2 7.1 fusion.23
  (219 shorter events, 79.7 us)
Async XLA Ops:
  7.2 1599.4 %copy-start = (bf16[768,768]{1,0:T(8,128)(2,1)S(1)}, bf16[768,768]{1,0:T(8,128)(2,1)}, u32[]{:S(2)}) copy-start(bf16[768,768]{1,0:T(8,128)(2,1)} %param.32) | copy-start | bytes 3538948
  7.2 1591.8 %all-reduce.8.cloned.1.call-start = ((), (), s32[]{:S(2)}) async-start(), calls=%async_computation | async-start | bytes 10223616 | tf_op jit(solution)/shard_map/psum | solution.py:131
  7.3 7.5 copy-start.45
  7.3 5.0 copy-start.58
  9.5 7.3 copy-start.51
  9.6 7.3 copy-start.52
  9.7 9.9 copy-start.37
  12.9 4.0 copy-start.41
  34.3 1361.8 %copy-start.16 = (bf16[8,208,3,64]{1,0,3,2:T(8,128)(2,1)}, bf16[8,208,3,64]{1,0,3,2:T(8,128)(2,1)S(1)}, u32[]{:S(2)}) copy-start(bf16[8,208,3,64]{1,0,3,2:T(8,128)(2,1)S(1)} %convert_element_type.154) | copy-start | bytes 1916932
  1294.0 102.1 %copy-start.9 = (f32[8,208,3,64]{1,0,3,2:T(8,128)S(1)}, f32[8,208,3,64]{1,0,3,2:T(8,128)}, u32[]{:S(2)}) copy-start(f32[8,208,3,64]{1,0,3,2:T(8,128)} %squeeze.8) | copy-start | bytes 3833860
  1413.0 394.8 %all-reduce.10.cloned.1.call-start = ((), (), s32[]{:S(2)}) async-start(), calls=%async_computation.1 | async-start | bytes 10223616 | tf_op jit(solution)/shard_map/psum | solution.py:162
  1606.6 6.7 copy-start.14
  1606.6 6.7 copy-start.12
  1606.6 6.7 copy-start.61
  1624.0 2222.9 %all-reduce.14.cloned.1.call-start = ((), (), s32[]{:S(2)}) async-start(), calls=%async_computation.3 | async-start | bytes 20447232 | tf_op jit(solution)/shard_map/psum | solution.py:140
  1807.8 5.4 copy-start.6
  1807.8 6.2 copy-start.8
  1814.0 8.2 copy-start.29
  1826.7 8.1 slice-start
  1830.4 4.4 slice-start.1
  1853.1 2069.2 %all-reduce.12.cloned.1.call-start = ((), (), s32[]{:S(2)}) async-start(), calls=%async_computation.2 | async-start | bytes 14155776 | tf_op jit(solution)/shard_map/psum | solution.py:234
  1861.2 5.7 copy-start.15
  1861.2 5.7 copy-start.22
  1870.9 4.1 copy-start.24
  1870.9 4.1 copy-start.36
  1904.2 1942.7 %copy-start.38 = (f32[1664]{0:T(1024)S(1)}, f32[1664]{0:T(1024)}, u32[]{:S(2)}) copy-start(f32[1664]{0:T(1024)} %copy-done.37) | copy-start | bytes 19972
  1904.2 1942.7 %copy-start.40 = (f32[1664]{0:T(1024)S(1)}, f32[1664]{0:T(1024)}, u32[]{:S(2)}) copy-start(f32[1664]{0:T(1024)} %copy-done.39) | copy-start | bytes 19972
  1904.2 1942.7 %copy-start.44 = (f32[768]{0:T(1024)S(1)}, f32[768]{0:T(1024)}, u32[]{:S(2)}) copy-start(f32[768]{0:T(1024)} %copy-done.43) | copy-start | bytes 9220
  3846.9 5.6 copy-start.7
  3846.9 5.6 copy-start.18
  3922.3 3.8 copy-start.28
  3926.1 3.9 copy-start.1
  (39 other events, 72.2 us)
Sparse Core Ops, SparseCore 0:
  1413.1 185.8 all-reduce.7
  1624.1 183.6 all-reduce.9
  1853.2 349.7 all-reduce.13
  2207.7 112.2 all-reduce.11
where the time goes:
time: 3970 us; the launch traced here: 3940 us
  other arithmetic  1930 us (49%)
  local copies, waits for them, and re-layouts  1500 us (38%)
  waiting for transfers between devices  358 us (9%)
  matrix products  68.2 us (2%)
  blocking collectives  57.1 us (1%)
    scatter-add x1, other arithmetic, body(): jax.ops.segment_sum(entries, flat_index, num_segments=table_size)  1870 us
    gather x2, local copies, waits for them, and re-layouts, body(): jnp.take(table_f, pair_index, axis=1)  1360 us
    psum x1, waiting for transfers between devices, body(): attn_branch = lax.psum(attn_part, 'narrow') + proj_bias.astype(float_type)  181 us
    psum x1, waiting for transfers between devices, body(): second_grad = lax.psum(second_part, 'narrow')  176 us
    reshape x2, local copies, waits for them, and re-layouts, body(): jnp.transpose(score_grad, (1, 0, 2, 3)).reshape(local_heads, -1)  86.9 us
  transfers between devices with their start and end apart: 4, of which 2 were waited for; matrix products, arithmetic and copies ran while one was open for 51% of the time, Pallas kernels for 0%

commit v1 on v0

--- a/solution.py
+++ b/solution.py
@@ -159,7 +159,8 @@
     up_bias_grad = jnp.sum(pre_low.astype(float_type), axis=0)
     up_weight_grad = jnp.einsum("rd,rf->df", second_in, pre_low, preferred_element_type=float_type)
     second_part = jnp.einsum("rf,df->rd", pre_low, up_weight, preferred_element_type=float_type)
-    second_grad = lax.psum(second_part, "narrow")
+    parts = lax.all_gather(second_part, "narrow")
+    second_grad = jnp.sum(parts, axis=0)
     second_gain_grad = jnp.sum(second_grad * normed_two, axis=0)
     second_shift_grad = jnp.sum(second_grad, axis=0)
     middle_grad = out_grad + norm_back(second_grad, normed_two, inv_two, second_gain_f)

time: 3970 us -> 4150 us (1.045)
  waiting for transfers between devices: 358 us -> 521 us
    all_gather x0 -> x1, waiting for transfers between devices: none -> 340 us  [body(): parts = lax.all_gather(second_part, 'narrow')]
    psum x1 -> x0, waiting for transfers between devices: 176 us -> none  [body(): second_grad = lax.psum(second_part, 'narrow')]
  transfers between devices with their start and end apart: 4 -> 4, of which waited for: 2 -> 2; matrix products, arithmetic and copies ran while one was open for 51% -> 49% of each run, Pallas kernels for 0% -> 0%
where the time goes in v1:
time: 4150 us; the launch traced here: 4110 us
  other arithmetic  1950 us (47%)
  local copies, waits for them, and re-layouts  1500 us (36%)
  waiting for transfers between devices  521 us (13%)
  matrix products  68.9 us (2%)
  blocking collectives  57 us (1%)
    scatter-add x1, other arithmetic, body(): jax.ops.segment_sum(entries, flat_index, num_segments=table_size)  1870 us
    gather x2, local copies, waits for them, and re-layouts, body(): jnp.take(table_f, pair_index, axis=1)  1350 us
    all_gather x1, waiting for transfers between devices, body(): parts = lax.all_gather(second_part, 'narrow')  340 us
    psum x1, waiting for transfers between devices, body(): attn_branch = lax.psum(attn_part, 'narrow') + proj_bias.astype(float_type)  181 us
    reshape x2, local copies, waits for them, and re-layouts, body(): jnp.transpose(score_grad, (1, 0, 2, 3)).reshape(local_heads, -1)  86.7 us
  transfers between devices with their start and end apart: 4, of which 2 were waited for; matrix products, arithmetic and copies ran while one was open for 49% of the time, Pallas kernels for 0%

profile of v1, /device:TPU:4, one launch (start us, length us, event | category | flops | bytes accessed | tf_op | source)
XLA Modules:
  0.0 4113.7 jit_solution(672316208479873606)
XLA Ops:
  34.3 3.5 squeeze.7
  41.0 1247.6 %gather_fusion = f32[346112,3]{1,0:T(8,128)} fusion(f32[3,2212]{0,1:T(8,128)S(1)} %copy.53, s32[346112]{0:T(1024)} %broadcast_clamp_fusion), kind=kCustom, calls=%fused_computation | custom fusion | bytes 9691136 | tf_op jit(solution)/shard_map/jit(_take)/gather | solution.py:100
  1288.5 102.1 %copy.55 = f32[8,208,208,3]{1,2,3,0:T(8,128)} copy(f32[8,208,208,3]{3,2,1,0:T(8,128)} %bitcast.9) | data formatting | bytes 8306688 | tf_op jit(solution)/shard_map/jit(_take)/gather | solution.py:100
  1390.6 5.6 fusion.61
  1403.3 4.2 fusion.65
  1408.3 3.8 multiply_convert_fusion.2
  1412.2 181.4 %all-reduce.7.cloned.1.call-done = f32[1664,768]{1,0:T(8,128)} async-done(((f32[1664,768]{1,0:T(8,128)}), f32[1664,768]{1,0:T(8,128)}) %all-reduce.7.cloned.1.call-update) | async-done | bytes 5111824 | tf_op jit(solution)/shard_map/psum | solution.py:131
  1593.5 4.2 fusion.60
  1601.2 6.7 multiply_convert_fusion.3
  1607.9 4.6 convert_reduce_fusion.1
  1614.1 4.5 fusion.67
  1619.9 6.6 fusion.66
  1626.5 339.6 %all-gather.3.cloned.1.call-done = f32[6656,768]{1,0:T(8,128)} async-done(((f32[1664,768]{1,0:T(8,128)}), f32[6656,768]{1,0:T(8,128)}) %all-gather.3.cloned.1.call-update) | async-done | bytes 20447248 | tf_op jit(solution)/shard_map/all_gather | solution.py:162
  1966.0 10.4 reduce_sum.207
  1976.4 6.0 multiply_reduce_fusion.2
  1982.7 5.9 multiply_reduce_fusion.3
  1995.4 3.7 convert_reduce_fusion.2
  1999.1 4.3 multiply_reduce_fusion.4
  2017.4 4.6 convolution_bitcast_fusion
  2030.1 5.7 fusion.69
  2035.7 3.8 fusion.68
  2039.8 4.1 fusion.39
  2047.9 8.8 fusion.6
  2056.7 6.2 copy.67
  2062.9 10.0 reshape.871
  2072.9 76.8 %copy.68 = f32[346112,3]{1,0:T(8,128)} copy(f32[346112,3]{0,1:T(4,128)} %bitcast.150) | data formatting | bytes 8306688 | tf_op jit(solution)/shard_map/reshape | solution.py:189
  2149.6 1865.8 %scatter_custom_fusion = f32[3,2212]{0,1:T(8,128)S(1)} fusion(s32[346112]{0:T(1024)S(1)} %reshape.872, f32[346112,3]{1,0:T(8,128)} %copy.68, f32[]{:T(128)} %constant.22.clone.1), kind=kCustom, calls=%fused_computation.92 | custom fusion | flops 1038336 | bytes 27056 | tf_op jit(solution)/shard_map/vmap()/scatter-add | solution.py:191
  4015.5 7.9 reduce_sum.222
  4023.5 5.6 fusion.24
  4029.1 5.1 multiply_reduce_fusion
  4034.2 57.0 %all-reduce = (f32[768]{0:T(1024)}, f32[768]{0:T(1024)}, f32[192]{0:T(256)}, f32[192]{0:T(256)}, f32[3,2212]{0,1:T(8,128)S(1)}, /*index=5*/f32[768]{0:T(1024)}, ...) all-reduce(f32[768]{0:T(1024)S(1)} %get-tuple-element.56, ...), channel_id=1, replica_groups=mesh['wide'=8,'narrow'=4] {'wide'}, use_global_device_ids=true, to_apply=%region_16.17 | all-reduce | flops 13932 | bytes 111456 | tf_op jit(solution)/shard_map/psum | solution.py:235
  4092.2 7.1 fusion.23
  (227 shorter events, 85.7 us)
Async XLA Ops:
  7.2 1594.0 %copy-start = (bf16[768,768]{1,0:T(8,128)(2,1)S(1)}, bf16[768,768]{1,0:T(8,128)(2,1)}, u32[]{:S(2)}) copy-start(bf16[768,768]{1,0:T(8,128)(2,1)} %param.32) | copy-start | bytes 3538948
  7.2 1586.3 %all-reduce.7.cloned.1.call-start = ((), (), s32[]{:S(2)}) async-start(), calls=%async_computation | async-start | bytes 10223616 | tf_op jit(solution)/shard_map/psum | solution.py:131
  7.3 7.5 copy-start.47
  7.3 5.0 copy-start.61
  9.5 7.3 copy-start.54
  9.6 7.3 copy-start.55
  9.7 9.9 copy-start.37
  12.9 4.0 copy-start.41
  34.3 1356.3 %copy-start.16 = (bf16[8,208,3,64]{1,0,3,2:T(8,128)(2,1)}, bf16[8,208,3,64]{1,0,3,2:T(8,128)(2,1)S(1)}, u32[]{:S(2)}) copy-start(bf16[8,208,3,64]{1,0,3,2:T(8,128)(2,1)S(1)} %convert_element_type.154) | copy-start | bytes 1916932
  1288.5 102.1 %copy-start.9 = (f32[8,208,3,64]{1,0,3,2:T(8,128)S(1)}, f32[8,208,3,64]{1,0,3,2:T(8,128)}, u32[]{:S(2)}) copy-start(f32[8,208,3,64]{1,0,3,2:T(8,128)} %squeeze.8) | copy-start | bytes 3833860
  1407.5 558.5 %all-gather.3.cloned.1.call-start = ((), (), s32[]{:S(2)}) async-start(), calls=%async_computation.1 | async-start | bytes 25559040 | tf_op jit(solution)/shard_map/all_gather | solution.py:162
  1601.2 6.7 copy-start.14
  1601.2 6.7 copy-start.12
  1601.2 6.7 copy-start.64
  1618.6 2404.8 %all-reduce.11.cloned.1.call-start = ((), (), s32[]{:S(2)}) async-start(), calls=%async_computation.3 | async-start | bytes 20447232 | tf_op jit(solution)/shard_map/psum | solution.py:140
  1976.4 6.0 copy-start.6
  1976.4 6.2 copy-start.7
  1982.7 8.3 copy-start.29
  1995.4 8.1 slice-start
  1999.1 4.4 slice-start.1
  2022.0 2077.2 %all-reduce.9.cloned.1.call-start = ((), (), s32[]{:S(2)}) async-start(), calls=%async_computation.2 | async-start | bytes 14155776 | tf_op jit(solution)/shard_map/psum | solution.py:235
  2030.1 5.7 copy-start.15
  2030.1 5.7 copy-start.22
  2039.8 4.1 copy-start.24
  2039.8 4.1 copy-start.36
  4015.5 7.9 copy-start.53
  4015.5 8.0 copy-start.38
  4015.5 8.0 copy-start.40
  4015.5 8.0 copy-start.44
  4023.5 5.6 copy-start.8
  4023.5 5.6 copy-start.18
  4023.5 5.6 copy-start.46
  (42 other events, 83.8 us)
Sparse Core Ops, SparseCore 0:
  1407.6 185.8 all-reduce.6
  1618.7 347.2 all-gather.2
  2022.2 349.3 all-reduce.10
  2376.3 112.2 all-reduce.8
